TPU v7x, 512 devices: a whole 4x4x16 slice. The times are simulated.
512 devices in a mesh: row: 32 (over z_lo, x, core), col: 16 (over y, z_hi).
Axes of the slice: x: 4, y: 4, z: 16 (z_hi: 4, z_lo: 4; z = z_hi * 4 + z_lo), core: 2. Of those that a mesh axis runs over, the one named last changes fastest.
Arguments:
- features: bfloat16 [65536, 512], P(('col', 'row')), may hold values from -6 to 6
- tile_values: bfloat16 [32, 16, 6, 256, 256], P('row', 'col'), may hold values from -0.109375 to 0.109375
- tile_index: int32 [32, 16, 6], P('row', 'col'), may hold values from 0 to 127, as said below
- tile_count: int32 [32, 16], P('row', 'col'), may hold values from 1 to 6, as said below
- weight: bfloat16 [512, 512], replicated, may hold values from -0.25 to 0.25
- cotangent: bfloat16 [65536, 512], P(('row', 'col')), may hold values from -6 to 6
Outputs:
- output: bfloat16 [65536, 512], P(('row', 'col'))
- weight_grad: float32 [512, 512], replicated
Inputs may be any that keep to these rules, and one draw needn't show every extreme that they name: `tile_index`: on each device the 6 slots hold different tile numbers. `tile_count`: some device has all 6 slots live.
All inputs are finite; a program needn't handle non-finite values.
Results may differ from a plain program's by a relative error of at most 0.024.
Values may be sent and summed in bfloat16 or wider, within the bound.
A program may use at most 64 MiB of HBM per device.

v0:
```python
import math
import jax
import jax.numpy as jnp
from jax import lax
from jax.sharding import PartitionSpec as P

F = 512
BLK = 256
RBG = 8
KMAX = 6


def local(features, tile_values, tile_index, tile_count, weight, cotangent):
    gathered = lax.all_gather(features, "row", axis=0, tiled=True)
    col_groups = gathered.shape[0] // BLK
    blocks = gathered.reshape(col_groups, BLK, F)
    tile_vals = tile_values[0, 0]
    tile_ids = tile_index[0, 0]
    live_count = tile_count[0, 0]
    row_slot = tile_ids // col_groups
    col_slot = tile_ids % col_groups
    is_live = jnp.arange(KMAX, dtype=jnp.int32) < live_count
    picked = blocks[col_slot]
    products = jnp.einsum("kab,kbf->kaf", tile_vals, picked, preferred_element_type=jnp.float32)
    placing = (
        (row_slot[:, None] == jnp.arange(RBG, dtype=jnp.int32)[None, :]) & is_live[:, None]
    ).astype(jnp.float32)
    partial_value = jnp.einsum("kr,kaf->raf", placing, products)
    rounded = partial_value.reshape(RBG * BLK, F).astype(jnp.bfloat16)
    summed = lax.psum_scatter(rounded, "col", scatter_dimension=0, tiled=True).astype(jnp.float32)
    aggregated = summed.astype(jnp.bfloat16)
    preact = jnp.dot(aggregated, weight, preferred_element_type=jnp.float32)
    output = jnp.where(preact > 0, preact, jnp.expm1(jnp.minimum(preact, 0.0))).astype(jnp.bfloat16)
    slope = jnp.where(preact > 0, 1.0, jnp.exp(jnp.minimum(preact, 0.0)))
    grad_pre = (cotangent.astype(jnp.float32) * slope).astype(jnp.bfloat16)
    grad_scale = 1.0 / math.sqrt(RBG * BLK * lax.axis_size("row"))
    local_grad = jnp.dot(aggregated.T, grad_pre, preferred_element_type=jnp.float32) * grad_scale
    weight_grad = lax.psum(local_grad, ("row", "col"))
    return (output, weight_grad)


def solution(mesh):
    placed = (
        P(("col", "row"), None),
        P("row", "col", None, None, None),
        P("row", "col", None),
        P("row", "col"),
        P(),
        P(("row", "col"), None),
    )
    return jax.shard_map(
        local, mesh=mesh, in_specs=placed, out_specs=(P(("row", "col"), None), P()), check_vma=False
    )
```

profile of v0, /device:TPU:1, one launch (start us, length us, event | category | flops | bytes accessed | tf_op | source)
XLA Modules:
  0.0 697.2 jit_solution(11324662987726796787)
XLA Ops:
  7.2 0.0 copy-start
  7.2 0.0 all-gather.2.cloned.1.call-start
  7.2 0.7 all-gather.2.cloned.1.call-update
  7.9 0.0 reduce-scatter.2.cloned.1.call-start
  8.6 0.7 fusion.19
  9.3 0.7 and_select_fusion.1
  10.0 74.0 %all-gather.2.cloned.1.call-done = bf16[4096,512]{1,0:T(8,128)(2,1)} async-done(((bf16[128,512]{1,0:T(8,128)(2,1)}), bf16[4096,512]{1,0:T(8,128)(2,1)}) %all-gather.2.cloned.1.call-update) | async-done | bytes 4194320 | tf_op jit(solution)/shard_map/all_gather | solution.py:14
  84.0 2.8 gather_fusion
  86.8 0.0 copy-done
  86.8 1.8 fusion.5
  88.7 3.3 copy.9
  91.9 0.7 fusion.2
  92.6 2.0 copy.8
  94.7 0.0 copy-start.1
  94.7 0.0 copy-start.2
  94.7 0.0 reduce-scatter.2.cloned.1.call-update
  94.7 0.0 all-reduce.2.cloned.1.call-start
  94.7 124.4 %reduce-scatter.2.cloned.1.call-done = bf16[128,512]{1,0:T(8,128)(2,1)} async-done(((bf16[2048,512]{1,0:T(8,128)(2,1)}), bf16[128,512]{1,0:T(8,128)(2,1)}) %reduce-scatter.2.cloned.1.call-update) | async-done | bytes 131088 | tf_op jit(solution)/shard_map/reduce_scatter | solution.py:30
  219.1 0.0 copy-done.1
  219.2 1.9 fusion.7
  221.0 0.0 copy-done.2
  221.0 2.2 convolution_multiply_fusion
  223.2 0.0 all-reduce.2.cloned.1.call-update
  223.3 465.1 %all-reduce.2.cloned.1.call-done = f32[512,512]{1,0:T(8,128)} async-done(((f32[512,512]{1,0:T(8,128)}), f32[512,512]{1,0:T(8,128)}) %all-reduce.2.cloned.1.call-update) | async-done | bytes 1048592 | tf_op jit(solution)/shard_map/psum | solution.py:38
  688.4 2.3 copy.12
  (2 shorter events, 0.0 us)
Async XLA Ops:
  7.2 79.7 %copy-start = (bf16[1,1,6,256,256]{4,3,2,1,0:T(8,128)(2,1)S(1)}, bf16[1,1,6,256,256]{4,3,2,1,0:T(8,128)(2,1)}, u32[]{:S(2)}) copy-start(bf16[1,1,6,256,256]{4,3,2,1,0:T(8,128)(2,1)} %param.7) | copy-start | bytes 2359300
  7.2 76.8 %all-gather.2.cloned.1.call-start = ((), (), s32[]{:S(2)}) async-start(), calls=%async_computation.1 | async-start | bytes 4325376 | tf_op jit(solution)/shard_map/all_gather | solution.py:14
  7.9 211.2 %reduce-scatter.2.cloned.1.call-start = ((), (), s32[]{:S(2)}) async-start(), calls=%async_computation.2 | async-start | bytes 2228224 | tf_op jit(solution)/shard_map/reduce_scatter | solution.py:30
  94.7 124.5 %copy-start.1 = (bf16[512,512]{1,0:T(8,128)(2,1)S(1)}, bf16[512,512]{1,0:T(8,128)(2,1)}, u32[]{:S(2)}) copy-start(bf16[512,512]{1,0:T(8,128)(2,1)} %param.10) | copy-start | bytes 1572868
  94.7 126.3 %copy-start.2 = (bf16[128,512]{1,0:T(8,128)(2,1)S(1)}, bf16[128,512]{1,0:T(8,128)(2,1)}, u32[]{:S(2)}) copy-start(bf16[128,512]{1,0:T(8,128)(2,1)} %param.11) | copy-start | bytes 393220
  94.7 593.7 %all-reduce.2.cloned.1.call-start = ((), (), s32[]{:S(2)}) async-start(), calls=%async_computation.3 | async-start | bytes 2097152 | tf_op jit(solution)/shard_map/psum | solution.py:38
Sparse Core Ops, SparseCore 0:
  10.2 73.7 all-gather.1
  94.8 124.2 reduce-scatter.1
  226.1 462.2 all-reduce.1
where the time goes:
time: 697 us
  waiting for transfers between devices  664 us (95%)
  between operations  14.4 us (2%)
  local copies, waits for them, and re-layouts  10.4 us (1%)
    psum x1, waiting for transfers between devices, local(): weight_grad = lax.psum(local_grad, ('row', 'col'))  465 us
    reduce_scatter x1, waiting for transfers between devices, local(): lax.psum_scatter(rounded, 'col', scatter_dimension=0, tiled=True)  124 us
    all_gather x1, waiting for transfers between devices, local(): gathered = lax.all_gather(features, 'row', axis=0, tiled=True)  74 us
  transfers between devices with their start and end apart: 3, of which 3 were waited for; matrix products, arithmetic and copies ran while one was open for 0% of the time, Pallas kernels for 0%

commit v1 on v0

--- a/solution.py
+++ b/solution.py
@@ -11,7 +11,9 @@
 
 
 def local(features, tile_values, tile_index, tile_count, weight, cotangent):
-    gathered = lax.all_gather(features, "row", axis=0, tiled=True)
+    gathered = jnp.concatenate(
+        lax.all_to_all(jnp.stack([features] * lax.axis_size("row")), "row", 0, 0), axis=0
+    )
     col_groups = gathered.shape[0] // BLK
     blocks = gathered.reshape(col_groups, BLK, F)
     tile_vals = tile_values[0, 0]

time: 697 us -> 732 us (1.050)
  waiting for transfers between devices: 664 us -> 685 us
  starting transfers between devices: 0.12 us -> 11.5 us
    all_to_all x0 -> x1, waiting for transfers between devices: none -> 92.6 us  [local(): lax.all_to_all(jnp.stack([features] * lax.axis_size('row')), 'row', 0, 0)]
    all_gather x1 -> x0, waiting for transfers between devices: 74 us -> none  [local(): gathered = lax.all_gather(features, 'row', axis=0, tiled=True)]
    all_to_all x0 -> x1, starting transfers between devices: none -> 11.5 us  [local(): lax.all_to_all(jnp.stack([features] * lax.axis_size('row')), 'row', 0, 0)]
where the time goes in v1:
time: 732 us
  waiting for transfers between devices  685 us (94%)
  between operations  14.8 us (2%)
  local copies, waits for them, and re-layouts  13.8 us (2%)
  starting transfers between devices  11.5 us (2%)
    psum x1, waiting for transfers between devices, local(): weight_grad = lax.psum(local_grad, ('row', 'col'))  465 us
    reduce_scatter x1, waiting for transfers between devices, local(): lax.psum_scatter(rounded, 'col', scatter_dimension=0, tiled=True)  127 us
    all_to_all x1, waiting for transfers between devices, local(): lax.all_to_all(jnp.stack([features] * lax.axis_size('row')), 'row', 0, 0)  92.6 us
  transfers between devices with their start and end apart: 3, of which 3 were waited for; matrix products, arithmetic and copies ran while one was open for 0% of the time, Pallas kernels for 0%

profile of v1, /device:TPU:1, one launch (start us, length us, event | category | flops | bytes accessed | tf_op | source)
XLA Modules:
  0.0 731.8 jit_solution(14700504031752219939)
XLA Ops:
  7.2 0.0 copy-start
  7.2 3.4 stack.2
  10.6 0.0 copy-start.3
  10.6 11.5 %all-to-all-start = ((bf16[32,128,512]{2,1,0:T(8,128)(2,1)}), bf16[32,128,512]{2,1,0:T(8,128)(2,1)}, u32[]{:S(2)}, u32[]{:S(2)}) async-start(bf16[32,128,512]{2,1,0:T(8,128)(2,1)} %stack.2), calls=%async_computation | async-start | bytes 8388608 | tf_op jit(solution)/shard_map/all_to_all | solution.py:15
  22.1 0.0 reduce-scatter.2.cloned.1.call-start
  22.8 0.0 copy-done.3
  22.8 92.6 %all-to-all-done = bf16[32,128,512]{2,1,0:T(8,128)(2,1)} async-done(((bf16[32,128,512]{2,1,0:T(8,128)(2,1)}), bf16[32,128,512]{2,1,0:T(8,128)(2,1)}, u32[]{:S(2)}, u32[]{:S(2)}) %all-to-all-start) | async-done | bytes 4194336 | tf_op jit(solution)/shard_map/all_to_all | solution.py:15
  115.5 2.8 gather_fusion
  118.3 0.0 copy-done
  118.3 1.8 fusion.5
  120.2 3.3 copy.9
  123.4 0.7 fusion.2
  124.1 2.0 copy.8
  126.2 0.0 copy-start.1
  126.2 0.0 copy-start.2
  126.2 0.0 reduce-scatter.2.cloned.1.call-update
  126.2 0.0 all-reduce.2.cloned.1.call-start
  126.2 127.3 %reduce-scatter.2.cloned.1.call-done = bf16[128,512]{1,0:T(8,128)(2,1)} async-done(((bf16[2048,512]{1,0:T(8,128)(2,1)}), bf16[128,512]{1,0:T(8,128)(2,1)}) %reduce-scatter.2.cloned.1.call-update) | async-done | bytes 131088 | tf_op jit(solution)/shard_map/reduce_scatter | solution.py:32
  253.5 0.0 copy-done.1
  253.5 1.9 fusion.7
  255.4 0.0 copy-done.2
  255.4 2.2 convolution_multiply_fusion
  257.6 0.0 all-reduce.2.cloned.1.call-update
  257.7 465.1 %all-reduce.2.cloned.1.call-done = f32[512,512]{1,0:T(8,128)} async-done(((f32[512,512]{1,0:T(8,128)}), f32[512,512]{1,0:T(8,128)}) %all-reduce.2.cloned.1.call-update) | async-done | bytes 1048592 | tf_op jit(solution)/shard_map/psum | solution.py:40
  722.7 2.3 copy.12
  (4 shorter events, 0.0 us)
Async XLA Ops:
  7.2 111.2 %copy-start = (bf16[1,1,6,256,256]{4,3,2,1,0:T(8,128)(2,1)S(1)}, bf16[1,1,6,256,256]{4,3,2,1,0:T(8,128)(2,1)}, u32[]{:S(2)}) copy-start(bf16[1,1,6,256,256]{4,3,2,1,0:T(8,128)(2,1)} %param.7) | copy-start | bytes 2359300
  10.6 12.2 %copy-start.3 = (s32[1,1,6]{2,1,0:T(1,128)S(1)}, s32[1,1,6]{2,1,0:T(1,128)}, u32[]{:S(2)}) copy-start(s32[1,1,6]{2,1,0:T(1,128)} %param.8) | copy-start | bytes 76
  10.6 104.9 %all-to-all-start = ((bf16[32,128,512]{2,1,0:T(8,128)(2,1)}), bf16[32,128,512]{2,1,0:T(8,128)(2,1)}, u32[]{:S(2)}, u32[]{:S(2)}) async-start(bf16[32,128,512]{2,1,0:T(8,128)(2,1)} %stack.2), calls=%async_computation | async-start | bytes 8388608 | tf_op jit(solution)/shard_map/all_to_all | solution.py:15
  22.1 231.5 %reduce-scatter.2.cloned.1.call-start = ((), (), s32[]{:S(2)}) async-start(), calls=%async_computation.2 | async-start | bytes 2228224 | tf_op jit(solution)/shard_map/reduce_scatter | solution.py:32
  126.2 127.4 %copy-start.1 = (bf16[512,512]{1,0:T(8,128)(2,1)S(1)}, bf16[512,512]{1,0:T(8,128)(2,1)}, u32[]{:S(2)}) copy-start(bf16[512,512]{1,0:T(8,128)(2,1)} %param.10) | copy-start | bytes 1572868
  126.2 129.3 %copy-start.2 = (bf16[128,512]{1,0:T(8,128)(2,1)S(1)}, bf16[128,512]{1,0:T(8,128)(2,1)}, u32[]{:S(2)}) copy-start(bf16[128,512]{1,0:T(8,128)(2,1)} %param.11) | copy-start | bytes 393220
  126.2 596.6 %all-reduce.2.cloned.1.call-start = ((), (), s32[]{:S(2)}) async-start(), calls=%async_computation.3 | async-start | bytes 2097152 | tf_op jit(solution)/shard_map/psum | solution.py:40
Sparse Core Ops, SparseCore 0:
  126.3 127.1 reduce-scatter.1
  260.5 462.2 all-reduce.1
